TPU v7x, 32 devices: a whole 2x2x4 slice. The times are simulated.
32 devices in a mesh: parts: 2 (over x), wide: 16 (over z, y, core).
Axes of the slice: x: 2, y: 2, z: 4, core: 2. Of those that a mesh axis runs over, the one named last changes fastest.
Arguments:
- tokens: bfloat16 [384, 7168], P(('parts', 'wide')), parts along dimension 0, may hold values from -6 to 6
- expert_ids: int32 [384, 8], P(('parts', 'wide')), parts along dimension 0, may hold values from 0 to 15, as said below
- gates: float32 [384, 8], P(('parts', 'wide')), parts along dimension 0, may hold values from 0.1 to 1
- w_gate: bfloat16 [2, 7168, 8192], P(None, None, 'wide'), may hold values from -0.0625 to 0.0625
- w_up: bfloat16 [2, 7168, 8192], P(None, None, 'wide'), may hold values from -0.0625 to 0.0625
- w_down: bfloat16 [2, 8192, 7168], P(None, 'wide'), may hold values from -0.1875 to 0.1875
Outputs:
- moe_out: bfloat16 [384, 7168], P(('parts', 'wide')), parts along dimension 0
There are 2 independent parts, one for each index of `parts`. A program takes and returns all parts, laid end to end along the dimension named above; an argument that names none is the same for every part. Nothing has to cross between parts.
Inputs may be any that keep to these rules, and one draw needn't show every extreme that they name: `expert_ids`: each row names the 2 experts g * 2 to g * 2 + 1 of each of 4 different groups g, in any order; in each part one group is named by every row.
All inputs are finite; a program needn't handle non-finite values.
Results may differ from a plain program's by a relative error of at most 0.0064.
Values may be sent and summed in bfloat16 or wider, within the bound.
A program may use at most 128 MiB of HBM per device.

v0:
```python
import jax
import jax.numpy as jnp
from jax import lax
from jax.sharding import PartitionSpec as P

GROUPS = 8
EXP_G = 2


def partner(block, axis, bit):
    count = lax.axis_size(axis)
    route = []
    for low in range(count):
        high = low | 1 << bit
        if high != low and high < count:
            route += [(low, high), (high, low)]
    return lax.ppermute(block, axis, route)


def route_table(expert_ids, gates):
    token_count = expert_ids.shape[0]
    catalog = jnp.arange(GROUPS * EXP_G, dtype=jnp.int32)
    picked = expert_ids[:, :, None] == catalog[None, None, :]
    weight_sum = jnp.sum(jnp.where(picked, gates[:, :, None], 0.0), axis=1)
    return weight_sum.astype(jnp.bfloat16).reshape(token_count, GROUPS, EXP_G)


def selection(expert_ids, wide_count, group_size, slot_count):
    token_count = expert_ids.shape[0]
    group_ids = jnp.arange(GROUPS, dtype=jnp.int32)
    member = jnp.any((expert_ids // EXP_G)[:, :, None] == group_ids[None, None, :], axis=1)
    position = jnp.cumsum(member.astype(jnp.int32), axis=0) - 1
    target = jnp.arange(wide_count, dtype=jnp.int32)
    target_group = (target // group_size)[:, None] == group_ids[None, :]
    target_rank = target % group_size
    member_dest = jnp.any(target_group[:, :, None] & member.T[None, :, :], axis=1)
    position_dest = jnp.sum(jnp.where(target_group[:, :, None], position.T[None, :, :], 0), axis=1)
    stride = token_count // slot_count
    wanted = (
        jnp.arange(slot_count, dtype=jnp.int32)[None, :] * stride + (target_rank % stride)[:, None]
    )
    chosen = member_dest[:, None, :] & (position_dest[:, None, :] == wanted[:, :, None])
    return (chosen, target_group)


def pack(tokens, route_weight, chosen, target_group):
    wide_count, slot_count, token_count = chosen.shape
    pick_table = chosen.astype(jnp.bfloat16).reshape(wide_count * slot_count, token_count)
    packed = jnp.dot(pick_table, tokens, preferred_element_type=jnp.float32).astype(jnp.bfloat16)
    packed = packed.reshape(wide_count, slot_count, tokens.shape[1])
    route_dest = jnp.einsum(
        "dg,tgj->dtj",
        target_group.astype(jnp.float32),
        route_weight.astype(jnp.float32),
        precision=lax.Precision.HIGHEST,
    )
    scaled = jnp.einsum(
        "dst,dtj->dsj", chosen.astype(jnp.float32), route_dest, precision=lax.Precision.HIGHEST
    )
    return (packed, scaled.astype(jnp.bfloat16))


def expert_block(inputs, scales, w_gate, w_up, w_down):
    summed = jnp.zeros((inputs.shape[0], w_down.shape[2]), jnp.float32)
    for expert in range(EXP_G):
        gate_value = jnp.dot(inputs, w_gate[expert], preferred_element_type=jnp.float32)
        lifted = jnp.dot(inputs, w_up[expert], preferred_element_type=jnp.float32)
        hidden = (jax.nn.silu(gate_value) * lifted).astype(jnp.bfloat16)
        summed = summed + scales[:, expert : expert + 1].astype(jnp.float32) * jnp.dot(
            hidden, w_down[expert], preferred_element_type=jnp.float32
        )
    return summed.astype(jnp.bfloat16)


def local(tokens, expert_ids, gates, w_gate, w_up, w_down):
    wide_count = lax.axis_size("wide")
    group_size = wide_count // GROUPS
    token_count = tokens.shape[0]
    model_width = tokens.shape[1]
    route_weight = route_table(expert_ids, gates)
    slot_count = token_count // group_size
    chosen, target_group = selection(expert_ids, wide_count, group_size, slot_count)
    packed, scaled = pack(tokens, route_weight, chosen, target_group)
    arrived, arrived_scale = (
        lax.all_to_all(packed, "wide", split_axis=0, concat_axis=0, tiled=True),
        lax.all_to_all(scaled, "wide", split_axis=0, concat_axis=0, tiled=True),
    )
    my_rank = lax.axis_index("wide") % group_size
    levels = group_size.bit_length() - 1
    held_rows = arrived[None]
    held_scale = arrived_scale[None]
    for level_index in range(levels):
        partner_rows, partner_scale = partner((held_rows, held_scale), "wide", level_index)
        upper_half = my_rank // (1 << level_index) % 2 == 1
        held_rows = jnp.concatenate(
            [
                jnp.where(upper_half, partner_rows, held_rows),
                jnp.where(upper_half, held_rows, partner_rows),
            ],
            0,
        )
        held_scale = jnp.concatenate(
            [
                jnp.where(upper_half, partner_scale, held_scale),
                jnp.where(upper_half, held_scale, partner_scale),
            ],
            0,
        )
    partial_value = expert_block(
        held_rows.reshape(-1, model_width), held_scale.reshape(-1, EXP_G), w_gate, w_up, w_down
    )
    partial_value = partial_value.reshape(group_size, wide_count, slot_count, model_width)
    returned = lax.all_to_all(partial_value, "wide", split_axis=1, concat_axis=1, tiled=True)
    chosen_grouped = chosen.reshape(GROUPS, group_size, slot_count, token_count).transpose(
        1, 0, 2, 3
    )
    pick_rows = jnp.broadcast_to(
        chosen_grouped[:, :, None], (group_size, GROUPS, group_size, slot_count, token_count)
    )
    pick_table = pick_rows.reshape(group_size * wide_count * slot_count, token_count).T.astype(
        jnp.bfloat16
    )
    output = jnp.dot(
        pick_table, returned.reshape(-1, model_width), preferred_element_type=jnp.float32
    )
    return output.astype(jnp.bfloat16)


def solution(mesh):
    return jax.shard_map(
        local,
        mesh=mesh,
        in_specs=(
            P(("parts", "wide"), None),
            P(("parts", "wide"), None),
            P(("parts", "wide"), None),
            P(None, None, "wide"),
            P(None, None, "wide"),
            P(None, "wide", None),
        ),
        out_specs=P(("parts", "wide"), None),
        check_vma=False,
    )
```

profile of v0, /device:TPU:15, one launch (start us, length us, event | category | flops | bytes accessed | tf_op | source)
XLA Modules:
  0.0 191.6 jit_solution(12496329950907122249)
XLA Ops:
  0.0 0.8 add_select_fusion
  0.8 0.2 reduce_window_sum.11
  1.7 0.1 and.129
  2.1 0.6 convolution_convert_fusion
  2.7 1.5 reshape.140
  4.2 6.5 %all-to-all-start.1 = ((bf16[16,6,7168]{2,1,0:T(8,128)(2,1)}), bf16[16,6,7168]{2,1,0:T(8,128)(2,1)S(1)}, u32[]{:S(2)}, u32[]{:S(2)}) async-start(bf16[16,6,7168]{2,1,0:T(8,128)(2,1)} %reshape.140), calls=%async_computation.1 | async-start | bytes 3670016 | tf_op jit(solution)/shard_map/all_to_all | solution.py:85
  10.9 0.1 select_reduce_fusion
  11.1 41.4 %all-to-all-done.1 = bf16[16,6,7168]{2,1,0:T(8,128)(2,1)S(1)} async-done(((bf16[16,6,7168]{2,1,0:T(8,128)(2,1)}), bf16[16,6,7168]{2,1,0:T(8,128)(2,1)S(1)}, u32[]{:S(2)}, u32[]{:S(2)}) %all-to-all-start.1) | async-done | bytes 1376288 | tf_op jit(solution)/shard_map/all_to_all | solution.py:85
  52.5 1.9 copy.64
  54.4 0.1 collective-permute-start.1
  54.6 0.2 fusion.34
  54.8 0.1 compare_and_fusion
  54.9 0.8 convolution_convert_fusion.2
  55.7 5.1 %all-to-all-start = ((bf16[16,6,2]{1,2,0:T(2,128)(2,1)}), bf16[16,6,2]{1,2,0:T(2,128)(2,1)S(1)}, u32[]{:S(2)}, u32[]{:S(2)}) async-start(bf16[16,6,2]{1,2,0:T(2,128)(2,1)} %convolution_convert_fusion.2), calls=%async_computation | async-start | bytes 16384 | tf_op jit(solution)/shard_map/all_to_all | solution.py:86
  60.7 3.8 %all-to-all-done = bf16[16,6,2]{1,2,0:T(2,128)(2,1)S(1)} async-done(((bf16[16,6,2]{1,2,0:T(2,128)(2,1)}), bf16[16,6,2]{1,2,0:T(2,128)(2,1)S(1)}, u32[]{:S(2)}, u32[]{:S(2)}) %all-to-all-start) | async-done | bytes 416 | tf_op jit(solution)/shard_map/all_to_all | solution.py:86
  64.5 0.7 collective-permute-start
  65.2 0.8 collective-permute-done
  66.1 0.1 reshape.139
  66.2 1.7 copy_select_fusion.1
  67.9 2.6 %pad_maximum_fusion = bf16[2,16,6,7168]{3,2,1,0:T(8,128)(2,1)} fusion(bf16[1,16,6,7168]{3,2,1,0:T(8,128)(2,1)S(1)} %get-tuple-element.6, bf16[1,16,6,7168]{3,2,1,0:T(8,128)(2,1)S(1)} %get-tuple-element.5), kind=kLoop, calls=%fused_computation.22 | loop fusion | flops 1376256 | bytes 5505024 | tf_op jit(solution)/shard_map/concatenate | solution.py:95
  70.5 3.2 %reshape.141 = bf16[192,7168]{1,0:T(8,128)(2,1)S(1)} reshape(bf16[2,16,6,7168]{3,2,1,0:T(8,128)(2,1)} %pad_maximum_fusion) | data formatting | bytes 5505024 | tf_op jit(solution)/shard_map/reshape | solution.py:110
  73.7 5.5 %fusion.3 = f32[192,512]{1,0:T(8,128)} fusion(bf16[192,7168]{1,0:T(8,128)(2,1)S(1)} %reshape.141, bf16[2,7168,512]{2,1,0:T(8,128)(2,1)} %param.10), kind=kOutput, calls=%fused_computation.7 | convolution fusion | flops 1409286144 | bytes 10485760 | tf_op jit(solution)/shard_map/dot_general | solution.py:67
  79.2 4.7 %fusion.8 = f32[192,512]{1,0:T(8,128)S(1)} fusion(bf16[192,7168]{1,0:T(8,128)(2,1)S(1)} %reshape.141, bf16[2,7168,512]{2,1,0:T(8,128)(2,1)} %param.10), kind=kOutput, calls=%fused_computation.12 | convolution fusion | flops 1409286144 | bytes 10485760 | tf_op jit(solution)/shard_map/dot_general | solution.py:67
  83.9 10.9 %convolution_multiply_fusion = f32[192,7168]{1,0:T(8,128)} fusion(bf16[2,512,7168]{2,1,0:T(8,128)(2,1)} %param.11, f32[192]{0:T(256)S(1)} %bitcast.69, f32[192,512]{1,0:T(8,128)} %fusion.3, bf16[192,7168]{1,0:T(8,128)(2,1)S(1)} %reshape.141, bf16[2,7168,512]{2,1,0:T(8,128)(2,1)} %param.9), kind=kOutput, calls=%fused_computation | convolution fusion | flops 2820538368 | bytes 23331584 | tf_op jit(solution)/shard_map/dot_general | solution.py:69
  94.8 11.4 %fusion.1 = bf16[192,7168]{1,0:T(8,128)(2,1)} fusion(f32[192,7168]{1,0:T(8,128)} %convolution_multiply_fusion, bf16[2,512,7168]{2,1,0:T(8,128)(2,1)} %param.11, f32[192]{0:T(256)S(1)} %bitcast.68, f32[192,512]{1,0:T(8,128)S(1)} %fusion.8, bf16[192,7168]{1,0:T(8,128)(2,1)S(1)} %reshape.141, bf16[2,7168,512]{2,1,0:T(8,128)(2,1)} %param.9), kind=kOutput, calls=%fused_computation.3 | convolution fusion | flops 2823290880 | bytes 26084096 | tf_op jit(solution)/shard_map/dot_general | solution.py:69
  106.2 4.6 %reshape.142 = bf16[2,16,6,7168]{3,2,1,0:T(8,128)(2,1)} reshape(bf16[192,7168]{1,0:T(8,128)(2,1)} %fusion.1) | data formatting | bytes 5505024 | tf_op jit(solution)/shard_map/reshape | solution.py:112
  110.8 6.4 %copy.67 = bf16[2,16,6,7168]{3,0,2,1:T(2,128)(2,1)} copy(bf16[2,16,6,7168]{3,2,1,0:T(8,128)(2,1)} %reshape.142) | data formatting | bytes 5505024 | tf_op jit(solution)/shard_map/reshape | solution.py:112
  117.2 5.9 %all-to-all-start.2 = ((bf16[2,16,6,7168]{3,0,2,1:T(2,128)(2,1)}), bf16[2,16,6,7168]{3,0,2,1:T(2,128)(2,1)S(1)}, u32[]{:S(2)}, u32[]{:S(2)}) async-start(bf16[2,16,6,7168]{3,0,2,1:T(2,128)(2,1)} %copy.67), calls=%async_computation.2 | async-start | bytes 5505024 | tf_op jit(solution)/shard_map/all_to_all | solution.py:113
  123.6 61.0 %all-to-all-done.2 = bf16[2,16,6,7168]{3,0,2,1:T(2,128)(2,1)S(1)} async-done(((bf16[2,16,6,7168]{3,0,2,1:T(2,128)(2,1)}), bf16[2,16,6,7168]{3,0,2,1:T(2,128)(2,1)S(1)}, u32[]{:S(2)}, u32[]{:S(2)}) %all-to-all-start.2) | async-done | bytes 2752544 | tf_op jit(solution)/shard_map/all_to_all | solution.py:113
  184.6 2.5 %copy.68 = bf16[2,16,6,7168]{3,2,1,0:T(8,128)(2,1)} copy(bf16[2,16,6,7168]{3,0,2,1:T(2,128)(2,1)S(1)} %all-to-all-done.2) | data formatting | bytes 5505024 | tf_op jit(solution)/shard_map/all_to_all | solution.py:113
  187.2 3.2 %reshape.143 = bf16[192,7168]{1,0:T(8,128)(2,1)S(1)} reshape(bf16[2,16,6,7168]{3,2,1,0:T(8,128)(2,1)} %copy.68) | data formatting | bytes 5505024 | tf_op jit(solution)/shard_map/reshape | solution.py:124
  190.4 1.2 convolution_convert_fusion.1
  (46 shorter events, 1.8 us)
Async XLA Ops:
  0.0 2.1 %copy-start = (bf16[12,7168]{1,0:T(8,128)(2,1)S(1)}, bf16[12,7168]{1,0:T(8,128)(2,1)}, u32[]{:S(2)}) copy-start(bf16[12,7168]{1,0:T(8,128)(2,1)} %param.6) | copy-start | bytes 516100
  2.6 8.1 %copy-start.2 = (s32[12,8]{0,1:T(8,128)S(1)}, s32[12,8]{0,1:T(8,128)}, u32[]{:S(2)}) copy-start(s32[12,8]{0,1:T(8,128)} %param.7) | copy-start | bytes 1156
  2.7 8.2 %copy-start.3 = (f32[12,8]{0,1:T(8,128)S(1)}, f32[12,8]{0,1:T(8,128)}, u32[]{:S(2)}) copy-start(f32[12,8]{0,1:T(8,128)} %param.8) | copy-start | bytes 1156
  4.2 48.3 %all-to-all-start.1 = ((bf16[16,6,7168]{2,1,0:T(8,128)(2,1)}), bf16[16,6,7168]{2,1,0:T(8,128)(2,1)S(1)}, u32[]{:S(2)}, u32[]{:S(2)}) async-start(bf16[16,6,7168]{2,1,0:T(8,128)(2,1)} %reshape.140), calls=%async_computation.1 | async-start | bytes 3670016 | tf_op jit(solution)/shard_map/all_to_all | solution.py:85
  54.4 11.8 %collective-permute-start.1 = (bf16[1,16,6,7168]{3,1,2,0:T(8,128)(2,1)}, bf16[1,16,6,7168]{3,1,2,0:T(8,128)(2,1)S(1)}, u32[]{:S(2)}, u32[]{:S(2)}) collective-permute-start(bf16[1,16,6,7168]{3,1,2,0:T(8,128)(2,1)} %copy.64), channel_id=1, source_target_pairs={{0,1},{1,0},{2,3},{3,2},{4,5},{5,4},{6,7},{7,6},{8,9},{9,8},{10,11... | collective-permute-start | bytes 4128776 | tf_op jit(solution)/shard_map/ppermute | solution.py:17
  55.7 8.9 %all-to-all-start = ((bf16[16,6,2]{1,2,0:T(2,128)(2,1)}), bf16[16,6,2]{1,2,0:T(2,128)(2,1)S(1)}, u32[]{:S(2)}, u32[]{:S(2)}) async-start(bf16[16,6,2]{1,2,0:T(2,128)(2,1)} %convolution_convert_fusion.2), calls=%async_computation | async-start | bytes 16384 | tf_op jit(solution)/shard_map/all_to_all | solution.py:86
  64.5 1.5 collective-permute-start
  117.2 67.4 %all-to-all-start.2 = ((bf16[2,16,6,7168]{3,0,2,1:T(2,128)(2,1)}), bf16[2,16,6,7168]{3,0,2,1:T(2,128)(2,1)S(1)}, u32[]{:S(2)}, u32[]{:S(2)}) async-start(bf16[2,16,6,7168]{3,0,2,1:T(2,128)(2,1)} %copy.67), calls=%async_computation.2 | async-start | bytes 5505024 | tf_op jit(solution)/shard_map/all_to_all | solution.py:113
  184.6 7.0 %copy-start.1 = (bf16[12,7168]{1,0:T(8,128)(2,1)S(1)}, bf16[12,7168]{1,0:T(8,128)(2,1)}, u32[]{:S(2)}) copy-start(bf16[12,7168]{1,0:T(8,128)(2,1)} %param.6) | copy-start | bytes 516100
where the time goes:
time: 192 us
  waiting for transfers between devices  107 us (56%)
  matrix products  35.2 us (18%)
  local copies, waits for them, and re-layouts  24.9 us (13%)
  starting transfers between devices  18.3 us (10%)
  other arithmetic  5.96 us (3%)
    all_to_all x1, waiting for transfers between devices, local(): lax.all_to_all(partial_value, 'wide', split_axis=1, concat_axis=1, tiled=...  61 us
    all_to_all x1, waiting for transfers between devices, local(): lax.all_to_all(packed, 'wide', split_axis=0, concat_axis=0, tiled=True)  41.4 us
    dot_general x2, matrix products, expert_block(): jnp.dot(hidden, w_down[expert], preferred_element_type=jnp.float32)  22.3 us
    reshape x2, local copies, waits for them, and re-layouts, local(): partial_value.reshape(group_size, wide_count, slot_count, model_width)  11 us
    dot_general x2, matrix products, expert_block(): lifted = jnp.dot(inputs, w_up[expert], preferred_element_type=jnp.float32)  10.1 us
    all_to_all x1, starting transfers between devices, local(): lax.all_to_all(packed, 'wide', split_axis=0, concat_axis=0, tiled=True)  6.52 us
    all_to_all x1, starting transfers between devices, local(): lax.all_to_all(partial_value, 'wide', split_axis=1, concat_axis=1, tiled=...  5.92 us
    all_to_all x1, starting transfers between devices, local(): lax.all_to_all(scaled, 'wide', split_axis=0, concat_axis=0, tiled=True)  5.06 us
  transfers between devices with their start and end apart: 5, of which 4 were waited for; matrix products, arithmetic and copies ran while one was open for 1% of the time, Pallas kernels for 0%

commit v1 on v0

--- a/solution.py
+++ b/solution.py
@@ -110,7 +110,10 @@
         held_rows.reshape(-1, model_width), held_scale.reshape(-1, EXP_G), w_gate, w_up, w_down
     )
     partial_value = partial_value.reshape(group_size, wide_count, slot_count, model_width)
-    returned = lax.all_to_all(partial_value, "wide", split_axis=1, concat_axis=1, tiled=True)
+    size = lax.axis_size("wide")
+    pieces = jnp.stack(jnp.split(partial_value, size, axis=1), axis=0)
+    pieces = lax.all_to_all(pieces, "wide", split_axis=0, concat_axis=0)
+    returned = jnp.concatenate(pieces, axis=1)
     chosen_grouped = chosen.reshape(GROUPS, group_size, slot_count, token_count).transpose(
         1, 0, 2, 3
     )

time: 192 us -> 206 us (1.073)
  local copies, waits for them, and re-layouts: 24.9 us -> 38.1 us
    unnamed x10 -> x25, local copies, waits for them, and re-layouts: 0.19 us -> 14.5 us
    another operation x0 -> x3, local copies, waits for them, and re-layouts: none -> 8.56 us  [the longest x2 5.34 us: local(): pieces = jnp.stack(jnp.split(partial_value, size, axis=1), axis=0)]
    reshape x2 -> x1, local copies, waits for them, and re-layouts: 11 us -> 4.61 us  [local(): partial_value.reshape(group_size, wide_count, slot_count, model_width)]
    all_to_all x1 -> x0, local copies, waits for them, and re-layouts: 2.53 us -> none  [local(): lax.all_to_all(partial_value, 'wide', split_axis=1, concat_axis=1, tiled=...]
where the time goes in v1:
time: 206 us; the launch traced here: 205 us
  waiting for transfers between devices  107 us (52%)
  local copies, waits for them, and re-layouts  38.1 us (18%)
  matrix products  35.2 us (17%)
  starting transfers between devices  18.3 us (9%)
  other arithmetic  5.96 us (3%)
    all_to_all x1, waiting for transfers between devices, local(): pieces = lax.all_to_all(pieces, 'wide', split_axis=0, concat_axis=0)  61 us
    all_to_all x1, waiting for transfers between devices, local(): lax.all_to_all(packed, 'wide', split_axis=0, concat_axis=0, tiled=True)  41.4 us
    dot_general x2, matrix products, expert_block(): jnp.dot(hidden, w_down[expert], preferred_element_type=jnp.float32)  22.3 us
    unnamed x25, local copies, waits for them, and re-layouts  14.5 us
    dot_general x2, matrix products, expert_block(): lifted = jnp.dot(inputs, w_up[expert], preferred_element_type=jnp.float32)  10.1 us
    all_to_all x1, starting transfers between devices, local(): lax.all_to_all(packed, 'wide', split_axis=0, concat_axis=0, tiled=True)  6.52 us
    all_to_all x1, starting transfers between devices, local(): pieces = lax.all_to_all(pieces, 'wide', split_axis=0, concat_axis=0)  5.92 us
    another operation x2, local copies, waits for them, and re-layouts, local(): pieces = jnp.stack(jnp.split(partial_value, size, axis=1), axis=0)  5.34 us
  transfers between devices with their start and end apart: 5, of which 4 were waited for; matrix products, arithmetic and copies ran while one was open for 1% of the time, Pallas kernels for 0%

profile of v1, /device:TPU:15, one launch (start us, length us, event | category | flops | bytes accessed | tf_op | source)
XLA Modules:
  0.0 204.9 jit_solution(1989519738851622746)
XLA Ops:
  2.7 1.5 reshape.140
  4.2 6.5 %all-to-all-start.1 = ((bf16[16,6,7168]{2,1,0:T(8,128)(2,1)}), bf16[16,6,7168]{2,1,0:T(8,128)(2,1)S(1)}, u32[]{:S(2)}, u32[]{:S(2)}) async-start(bf16[16,6,7168]{2,1,0:T(8,128)(2,1)} %reshape.140), calls=%async_computation.1 | async-start | bytes 3670016 | tf_op jit(solution)/shard_map/all_to_all | solution.py:85
  11.1 41.4 %all-to-all-done.1 = bf16[16,6,7168]{2,1,0:T(8,128)(2,1)S(1)} async-done(((bf16[16,6,7168]{2,1,0:T(8,128)(2,1)}), bf16[16,6,7168]{2,1,0:T(8,128)(2,1)S(1)}, u32[]{:S(2)}, u32[]{:S(2)}) %all-to-all-start.1) | async-done | bytes 1376288 | tf_op jit(solution)/shard_map/all_to_all | solution.py:85
  52.5 1.9 copy.126
  55.7 5.1 %all-to-all-start = ((bf16[16,6,2]{1,2,0:T(2,128)(2,1)}), bf16[16,6,2]{1,2,0:T(2,128)(2,1)S(1)}, u32[]{:S(2)}, u32[]{:S(2)}) async-start(bf16[16,6,2]{1,2,0:T(2,128)(2,1)} %convolution_convert_fusion.2), calls=%async_computation | async-start | bytes 16384 | tf_op jit(solution)/shard_map/all_to_all | solution.py:86
  60.7 3.8 %all-to-all-done = bf16[16,6,2]{1,2,0:T(2,128)(2,1)S(1)} async-done(((bf16[16,6,2]{1,2,0:T(2,128)(2,1)}), bf16[16,6,2]{1,2,0:T(2,128)(2,1)S(1)}, u32[]{:S(2)}, u32[]{:S(2)}) %all-to-all-start) | async-done | bytes 416 | tf_op jit(solution)/shard_map/all_to_all | solution.py:86
  66.2 1.7 copy_select_fusion.1
  67.9 2.6 %pad_maximum_fusion = bf16[2,16,6,7168]{3,2,1,0:T(8,128)(2,1)} fusion(bf16[1,16,6,7168]{3,2,1,0:T(8,128)(2,1)S(1)} %get-tuple-element.6, bf16[1,16,6,7168]{3,2,1,0:T(8,128)(2,1)S(1)} %get-tuple-element.5), kind=kLoop, calls=%fused_computation.22 | loop fusion | flops 1376256 | bytes 5505024 | tf_op jit(solution)/shard_map/concatenate | solution.py:95
  70.5 3.2 %reshape.141 = bf16[192,7168]{1,0:T(8,128)(2,1)S(1)} reshape(bf16[2,16,6,7168]{3,2,1,0:T(8,128)(2,1)} %pad_maximum_fusion) | data formatting | bytes 5505024 | tf_op jit(solution)/shard_map/reshape | solution.py:110
  73.7 5.5 %fusion.3 = f32[192,512]{1,0:T(8,128)} fusion(bf16[192,7168]{1,0:T(8,128)(2,1)S(1)} %reshape.141, bf16[2,7168,512]{2,1,0:T(8,128)(2,1)} %param.10), kind=kOutput, calls=%fused_computation.7 | convolution fusion | flops 1409286144 | bytes 10485760 | tf_op jit(solution)/shard_map/dot_general | solution.py:67
  79.2 4.7 %fusion.8 = f32[192,512]{1,0:T(8,128)S(1)} fusion(bf16[192,7168]{1,0:T(8,128)(2,1)S(1)} %reshape.141, bf16[2,7168,512]{2,1,0:T(8,128)(2,1)} %param.10), kind=kOutput, calls=%fused_computation.12 | convolution fusion | flops 1409286144 | bytes 10485760 | tf_op jit(solution)/shard_map/dot_general | solution.py:67
  83.9 10.9 %convolution_multiply_fusion = f32[192,7168]{1,0:T(8,128)} fusion(bf16[2,512,7168]{2,1,0:T(8,128)(2,1)} %param.11, f32[192]{0:T(256)S(1)} %bitcast.167, f32[192,512]{1,0:T(8,128)} %fusion.3, bf16[192,7168]{1,0:T(8,128)(2,1)S(1)} %reshape.141, bf16[2,7168,512]{2,1,0:T(8,128)(2,1)} %param.9), kind=kOutput, calls=%fused_computation | convolution fusion | flops 2820538368 | bytes 23331584 | tf_op jit(solution)/shard_map/dot_general | solution.py:69
  94.8 11.4 %fusion.1 = bf16[192,7168]{1,0:T(8,128)(2,1)} fusion(f32[192,7168]{1,0:T(8,128)} %convolution_multiply_fusion, bf16[2,512,7168]{2,1,0:T(8,128)(2,1)} %param.11, f32[192]{0:T(256)S(1)} %bitcast.166, f32[192,512]{1,0:T(8,128)S(1)} %fusion.8, bf16[192,7168]{1,0:T(8,128)(2,1)S(1)} %reshape.141, bf16[2,7168,512]{2,1,0:T(8,128)(2,1)} %param.9), kind=kOutput, calls=%fused_computation.3 | convolution fusion | flops 2823290880 | bytes 26084096 | tf_op jit(solution)/shard_map/dot_general | solution.py:69
  106.2 4.6 %reshape.142 = bf16[2,16,6,7168]{3,2,1,0:T(8,128)(2,1)} reshape(bf16[192,7168]{1,0:T(8,128)(2,1)} %fusion.1) | data formatting | bytes 5505024 | tf_op jit(solution)/shard_map/reshape | solution.py:112
  111.8 1.0 fusion.32
  112.7 1.0 fusion.31
  113.7 1.0 fusion.30
  114.7 1.0 fusion.29
  115.6 1.0 fusion.28
  116.6 1.0 fusion.27
  117.5 1.0 fusion.26
  118.5 1.0 fusion.25
  119.4 1.0 fusion.24
  120.4 1.0 fusion.23
  121.4 1.0 fusion.22
  123.3 1.0 fusion.20
  126.2 4.4 %copy.144 = bf16[16,2,1,6,7168]{4,1,3,2,0:T(2,128)(2,1)} copy(bf16[16,2,1,6,7168]{4,3,1,2,0:T(8,128)(2,1)S(1)} %fusion.18) | data formatting | bytes 5505024 | tf_op jit(solution)/shard_map/stack | solution.py:114
  130.5 5.9 %all-to-all-start.2 = ((bf16[16,2,1,6,7168]{4,1,3,2,0:T(2,128)(2,1)}), bf16[16,2,1,6,7168]{4,1,3,2,0:T(2,128)(2,1)S(1)}, u32[]{:S(2)}, u32[]{:S(2)}) async-start(bf16[16,2,1,6,7168]{4,1,3,2,0:T(2,128)(2,1)} %copy.144), calls=%async_computation.2 | async-start | bytes 5505024 | tf_op jit(solution)/shard_map/all_to_all | solution.py:115
  136.9 61.0 %all-to-all-done.2 = bf16[16,2,1,6,7168]{4,1,3,2,0:T(2,128)(2,1)S(1)} async-done(((bf16[16,2,1,6,7168]{4,1,3,2,0:T(2,128)(2,1)}), bf16[16,2,1,6,7168]{4,1,3,2,0:T(2,128)(2,1)S(1)}, u32[]{:S(2)}, u32[]{:S(2)}) %all-to-all-start.2) | async-done | bytes 2752544 | tf_op jit(solution)/shard_map/all_to_all | solution.py:115
  197.9 2.5 %copy.145 = bf16[2,16,1,6,7168]{4,3,1,0,2:T(8,128)(2,1)} copy(bf16[2,16,1,6,7168]{4,0,3,2,1:T(2,128)(2,1)S(1)} %bitcast.160) | data formatting | bytes 5505024 | tf_op jit(solution)/shard_map/reshape | solution.py:116
  200.5 3.2 %reshape_reshape.3 = bf16[192,7168]{1,0:T(8,128)(2,1)S(1)} reshape(bf16[2,16,1,6,7168]{4,3,1,0,2:T(8,128)(2,1)} %copy.145) | data formatting | bytes 5505024 | tf_op jit(solution)/shard_map/reshape;reshape | solution.py:127
  203.7 1.2 convolution_convert_fusion.1
  (62 shorter events, 10.1 us)
Async XLA Ops:
  0.0 2.1 %copy-start = (bf16[12,7168]{1,0:T(8,128)(2,1)S(1)}, bf16[12,7168]{1,0:T(8,128)(2,1)}, u32[]{:S(2)}) copy-start(bf16[12,7168]{1,0:T(8,128)(2,1)} %param.6) | copy-start | bytes 516100
  2.6 8.1 %copy-start.2 = (s32[12,8]{0,1:T(8,128)S(1)}, s32[12,8]{0,1:T(8,128)}, u32[]{:S(2)}) copy-start(s32[12,8]{0,1:T(8,128)} %param.7) | copy-start | bytes 1156
  2.7 8.2 %copy-start.3 = (f32[12,8]{0,1:T(8,128)S(1)}, f32[12,8]{0,1:T(8,128)}, u32[]{:S(2)}) copy-start(f32[12,8]{0,1:T(8,128)} %param.8) | copy-start | bytes 1156
  4.2 48.3 %all-to-all-start.1 = ((bf16[16,6,7168]{2,1,0:T(8,128)(2,1)}), bf16[16,6,7168]{2,1,0:T(8,128)(2,1)S(1)}, u32[]{:S(2)}, u32[]{:S(2)}) async-start(bf16[16,6,7168]{2,1,0:T(8,128)(2,1)} %reshape.140), calls=%async_computation.1 | async-start | bytes 3670016 | tf_op jit(solution)/shard_map/all_to_all | solution.py:85
  54.4 11.8 %collective-permute-start.1 = (bf16[1,16,6,7168]{3,1,2,0:T(8,128)(2,1)}, bf16[1,16,6,7168]{3,1,2,0:T(8,128)(2,1)S(1)}, u32[]{:S(2)}, u32[]{:S(2)}) collective-permute-start(bf16[1,16,6,7168]{3,1,2,0:T(8,128)(2,1)} %copy.126), channel_id=1, source_target_pairs={{0,1},{1,0},{2,3},{3,2},{4,5},{5,4},{6,7},{7,6},{8,9},{9,8},{10,11... | collective-permute-start | bytes 4128776 | tf_op jit(solution)/shard_map/ppermute | solution.py:17
  55.7 8.9 %all-to-all-start = ((bf16[16,6,2]{1,2,0:T(2,128)(2,1)}), bf16[16,6,2]{1,2,0:T(2,128)(2,1)S(1)}, u32[]{:S(2)}, u32[]{:S(2)}) async-start(bf16[16,6,2]{1,2,0:T(2,128)(2,1)} %convolution_convert_fusion.2), calls=%async_computation | async-start | bytes 16384 | tf_op jit(solution)/shard_map/all_to_all | solution.py:86
  64.5 1.5 collective-permute-start
  130.5 67.4 %all-to-all-start.2 = ((bf16[16,2,1,6,7168]{4,1,3,2,0:T(2,128)(2,1)}), bf16[16,2,1,6,7168]{4,1,3,2,0:T(2,128)(2,1)S(1)}, u32[]{:S(2)}, u32[]{:S(2)}) async-start(bf16[16,2,1,6,7168]{4,1,3,2,0:T(2,128)(2,1)} %copy.144), calls=%async_computation.2 | async-start | bytes 5505024 | tf_op jit(solution)/shard_map/all_to_all | solution.py:115
  197.9 7.0 %copy-start.1 = (bf16[12,7168]{1,0:T(8,128)(2,1)S(1)}, bf16[12,7168]{1,0:T(8,128)(2,1)}, u32[]{:S(2)}) copy-start(bf16[12,7168]{1,0:T(8,128)(2,1)} %param.6) | copy-start | bytes 516100
